TPU v7x, 32 devices: a whole 2x2x4 slice. The times are simulated.
32 devices in a mesh: grp: 2 (over core), zon: 8 (over z, y), mer: 2 (over x).
Axes of the slice: x: 2, y: 2, z: 4, core: 2. Of those that a mesh axis runs over, the one named last changes fastest.
Arguments:
- model_state: float32 [4, 6, 128, 1024], P(None, 'grp', 'mer', 'zon'), may hold values from -4 to 4
- control: float32 [4, 6, 128, 1024], P('grp', None, 'mer', 'zon'), may hold values from -6 to 6
- error_std: float32 [4, 6, 128, 1024], P('grp', None, 'mer', 'zon'), may hold values from 0.3 to 3
- bottom_level: int32 [128, 1024], P('mer', 'zon'), may hold values from 0 to 6
- obs_count: int32 [2, 2, 8], P('grp', 'mer', 'zon'), may hold values from 1 to 256, as said below
- obs_corner: int32 [2, 2, 8, 256], P('grp', 'mer', 'zon'), may hold values from 0 to 98174, as said below
- obs_weight: float32 [2, 2, 8, 4, 256], P('grp', 'mer', 'zon'), may hold values from 0 to 1, as said below
- obs_value: float32 [2, 2, 8, 256], P('grp', 'mer', 'zon'), may hold values from -5 to 5
- obs_precision: float32 [2, 2, 8, 256], P('grp', 'mer', 'zon'), may hold values from 0.25 to 4
Outputs:
- gradient: float32 [4, 6, 128, 1024], P('grp', None, 'mer', 'zon')
Inputs may be any that keep to these rules, and one draw needn't show every extreme that they name: `obs_count`: at least one live observation in every block, exactly 256 in some block. `obs_corner`: each slot's four interpolation cells lie in its own tile; padded slots also hold valid indices. `obs_weight`: the four weights of a slot are nonnegative and sum to one.
All inputs are finite; a program needn't handle non-finite values.
Results may differ from a plain program's by a relative error of at most 0.0003.
Values may be sent and summed in bfloat16 or wider, within the bound.
A program may use at most 64 MiB of HBM per device.

v0:
```python
import functools

import jax
import jax.numpy as jnp
from jax import lax
from jax.experimental import pallas as pl
from jax.experimental.pallas import tpu as pltpu
from jax.sharding import PartitionSpec as P

SWEEPS = 10
SMOOTHING = 0.2
ADVECTION = 0.1
MIXING = 0.15

MESH = pl.DeviceIdType.MESH
PAD = 16
ZONAL = [(1, 0), (-1, 0)]
MERIDIONAL = [(0, 1), (0, -1)]
SIDES = ZONAL + MERIDIONAL
DIRS = [(1, 1), (1, -1), (-1, 1), (-1, -1)] + ZONAL + MERIDIONAL


def pieces(value):
    parts = []
    for _ in range(2):
        part = value.astype(jnp.bfloat16)
        parts.append(part)
        value = value - part.astype(jnp.float32)
    return parts


def kernel(
    sizes,
    state_hbm,
    control_hbm,
    std_hbm,
    bottom_hbm,
    count_hbm,
    corner_hbm,
    weight_hbm,
    value_hbm,
    precision_hbm,
    out_ref,
    bottom_ref,
    count_ref,
    corner_ref,
    weight_ref,
    value_ref,
    precision_ref,
    state,
    state_rows,
    state_rows_in,
    state_cols,
    state_cols_in,
    back,
    back_in,
    field,
    turned_in,
    strips_out,
    strips,
    field_two,
    strips_out_two,
    strips_two,
    fold_ref,
    turned_out,
    depth_ref,
    ping,
    pong,
    bottom,
    bottom_side,
    keep_ref,
    gain_ref,
    std,
    smooth_ref,
    x_ref,
    rows_hot,
    rows_hot_t,
    obs_stack,
    corner_hot,
    local_sem,
    bot_send,
    bot_recv,
    st_send,
    st_recv,
    one_send,
    one_recv,
    two_send,
    two_recv,
    bg_send,
    bg_recv,
):
    n_zon, n_mer, levels, half, pair, fields, R, C = sizes
    w = SWEEPS
    planes = pair * levels
    tiles = (R + 2 * w + 7) // 8
    base = PAD - (8 * tiles - R) // 2
    columns = (C + 2 * w + 7) // 8
    column_base = PAD - (8 * columns - C) // 2
    g = lax.axis_index("grp")
    z = lax.axis_index("zon")
    m = lax.axis_index("mer")
    has = {-1: m > 0, 1: m < n_mer - 1}

    def device(dz, dm):
        return (g, lax.rem(z + dz + n_zon, n_zon), m + dm)

    def when(dm, action):
        if dm == 0:
            action()
        else:
            pl.when(has[dm])(action)

    barrier = pltpu.get_barrier_semaphore()
    pl.semaphore_signal(barrier, inc=1, device_id=(1 - g, z, m), device_id_type=MESH)
    for dz, dm in DIRS:
        def greet(dz=dz, dm=dm):
            pl.semaphore_signal(barrier, inc=1, device_id=device(dz, dm), device_id_type=MESH)
        when(dm, greet)

    load_control = pltpu.make_async_copy(control_hbm, field.at[:, pl.ds(PAD, R)], local_sem.at[0])
    load_state = pltpu.make_async_copy(state_hbm, state.at[:, pl.ds(8, R)], local_sem.at[1])
    load_std = pltpu.make_async_copy(std_hbm, std, local_sem.at[2])
    load_bottom = pltpu.make_async_copy(bottom_hbm, bottom_ref, local_sem.at[3])
    tables = [
        pltpu.make_async_copy(source, target, local_sem.at[4 + i])
        for i, (source, target) in enumerate([
            (count_hbm, count_ref),
            (corner_hbm, corner_ref),
            (weight_hbm, weight_ref),
            (value_hbm, value_ref),
            (precision_hbm, precision_ref),
        ])
    ]
    load_bottom.start()
    load_state.start()
    load_control.start()
    load_std.start()
    for table in tables:
        table.start()

    lane_r = lax.broadcasted_iota(jnp.int32, (R, C), 1)
    lane = lax.broadcasted_iota(jnp.int32, (8, C), 1)
    lane_pad = lax.broadcasted_iota(jnp.int32, (PAD, C), 1)

    def pack(source, target):
        def one(p, carry):
            first, last = carry
            u = source[p, pl.ds(PAD, R), :]
            here = (lane_r >= p * w) & (lane_r < p * w + w)
            last = jnp.where(here, pltpu.roll(u, lax.rem(p * w + w, C), axis=1), last)
            first = jnp.where(here, pltpu.roll(u, lax.rem(p * w, C), axis=1), first)
            return first, last
        zero = jnp.zeros((R, C), jnp.float32)
        first, last = lax.fori_loop(0, planes, one, (zero, zero))
        target[0] = last
        target[1] = first

    def span(dm):
        if dm == 0:
            return pl.ds(0, R), pl.ds(PAD, R)
        if dm == 1:
            return pl.ds(R - PAD, PAD), pl.ds(0, PAD)
        return pl.ds(0, PAD), pl.ds(PAD + R, PAD)

    def side(dz):
        return 0 if dz == 1 else 1

    def bottom_copy(i):
        dz, dm = DIRS[i]
        src, dst = span(dm)
        target = bottom.at[dst] if dz == 0 else bottom_side.at[side(dz), dst]
        return pltpu.make_async_remote_copy(
            src_ref=bottom_ref.at[src], dst_ref=target,
            send_sem=bot_send.at[i], recv_sem=bot_recv.at[i],
            device_id=device(dz, dm), device_id_type=MESH)

    def halo_copy(i, whole, packed, landed, send, recv):
        dz, dm = DIRS[i]
        src, dst = span(dm)
        if dz == 0:
            inner = pl.ds(PAD + R - w, w) if dm == 1 else pl.ds(PAD, w)
            outer = pl.ds(PAD - w, w) if dm == 1 else pl.ds(PAD + R, w)
            source, target = whole.at[:, inner], whole.at[:, outer]
        else:
            source, target = packed.at[side(dz), src], landed.at[side(dz), dst]
        return pltpu.make_async_remote_copy(
            src_ref=source, dst_ref=target, send_sem=send.at[i], recv_sem=recv.at[i],
            device_id=device(dz, dm), device_id_type=MESH)

    def one_copy(i):
        return halo_copy(i, field, strips_out, strips, one_send, one_recv)

    def two_copy(i):
        return halo_copy(i, field_two, strips_out_two, strips_two, two_send, two_recv)

    def state_copy(i):
        dz, dm = SIDES[i]
        if dz == 0:
            k = 0 if dm == 1 else 1
            source, target = state_rows.at[k], state_rows_in.at[k]
        else:
            source, target = state_cols.at[side(dz)], state_cols_in.at[side(dz)]
        return pltpu.make_async_remote_copy(
            src_ref=source, dst_ref=target, send_sem=st_send.at[i], recv_sem=st_recv.at[i],
            device_id=device(dz, dm), device_id_type=MESH)

    def start_all(copies, make):
        for i, (dz, dm) in enumerate(copies):
            when(dm, lambda i=i: make(i).start())

    def land_all(copies, make):
        for i, (dz, dm) in enumerate(copies):
            when(-dm, lambda i=i: make(i).wait_recv())

    def sent_all(copies, make):
        for i, (dz, dm) in enumerate(copies):
            when(dm, lambda i=i: make(i).wait_send())

    load_bottom.wait()
    bottom[pl.ds(PAD, R)] = bottom_ref[...]
    for dm, rows in ((-1, pl.ds(0, PAD)), (1, pl.ds(PAD + R, PAD))):
        def dry(rows=rows):
            empty = jnp.zeros((PAD, C), jnp.int32)
            bottom[rows] = empty
            bottom_side[0, rows] = empty
            bottom_side[1, rows] = empty
        pl.when(jnp.logical_not(has[dm]))(dry)

    load_state.wait()
    first = jnp.zeros((R, C), jnp.float32)
    last = jnp.zeros((R, C), jnp.float32)
    for q in range(fields * half):
        u = state[q, pl.ds(8, R), :]
        last = jnp.where(lane_r == q, pltpu.roll(u, (q + 1) % C, axis=1), last)
        first = jnp.where(lane_r == q, pltpu.roll(u, q, axis=1), first)
        state_rows[0, pl.ds(q, 1), :] = state[q, pl.ds(8 + R - 1, 1), :]
        state_rows[1, pl.ds(q, 1), :] = state[q, pl.ds(8, 1), :]
    state_cols[0] = last
    state_cols[1] = first

    edges = jnp.where(has[-1], 1, 0) + jnp.where(has[1], 1, 0)
    load_control.wait()
    pack(field, strips_out)
    pl.semaphore_wait(barrier, 3 + 3 * edges)
    start_all(DIRS, bottom_copy)
    start_all(SIDES, state_copy)
    start_all(DIRS, one_copy)

    for table in tables:
        table.wait()
    shift = C.bit_length() - 1
    slots = corner_ref.shape[1]
    corner = corner_ref[...]
    flat_row = lax.shift_right_logical(corner, jnp.full_like(corner, shift))
    column = corner - flat_row * C
    live = (lax.broadcasted_iota(jnp.int32, (1, slots), 1) < count_ref[...]).astype(jnp.float32)
    obs_stack[...] = jnp.zeros_like(obs_stack)
    obs_stack[pl.ds(0, 1), :] = column.astype(jnp.float32)
    obs_stack[pl.ds(1, 1), :] = flat_row.astype(jnp.float32)
    obs_stack[pl.ds(2, 4), :] = weight_ref[...]
    obs_stack[pl.ds(6, 1), :] = live * precision_ref[...]
    obs_stack[pl.ds(7, 1), :] = value_ref[...]
    turned = jnp.transpose(obs_stack[...])
    col_i = turned[:, 0:1].astype(jnp.int32)
    col_row = turned[:, 1:2].astype(jnp.int32)
    lane_s = lax.broadcasted_iota(jnp.int32, (slots, C), 1)
    here = lane_s == col_i
    beside = lane_s == col_i + 1
    for k in range(2):
        corner_hot[:, k * C:(k + 1) * C] = jnp.where(
            here, turned[:, 2 + 2 * k:3 + 2 * k], 0.0
        ) + jnp.where(beside, turned[:, 3 + 2 * k:4 + 2 * k], 0.0)
    scale = turned[:, 6:7]
    seen = turned[:, 7:8]
    for k in range(planes * R // C):
        ids = lax.broadcasted_iota(jnp.int32, (slots, C), 1) + k * C
        rows_hot[:, k * C:(k + 1) * C] = jnp.where(ids == col_row, 1.0, 0.0).astype(jnp.bfloat16)
        ids = lax.broadcasted_iota(jnp.int32, (C, slots), 0) + k * C
        rows_hot_t[k * C:(k + 1) * C, :] = jnp.where(ids == flat_row, 1.0, 0.0).astype(jnp.bfloat16)

    def strided(t):
        return pl.ds(base + t, 8, tiles)

    def strided_column(k):
        return pl.ds(column_base + k, 8, columns)

    spare = jnp.zeros((C - 8 * planes, C), jnp.float32)

    def turn(source, target):
        for t in range(tiles):
            rows = [source[p, strided(t), :] for p in range(planes)]
            target[t, pl.ds(PAD, C), :] = jnp.transpose(jnp.concatenate(rows + [spare], axis=0))

    def turn_back(target):
        for t in range(tiles):
            rows = jnp.transpose(turned_out[t, pl.ds(PAD, C), :])
            for p in range(planes):
                target[p, strided(t), :] = rows[8 * p:8 * p + 8]

    def unfold(landed, target):
        group = lax.shift_right_logical(lane_pad, jnp.full_like(lane_pad, 3))
        for h in range(2):
            rows = [landed[h, strided(t), :] for t in range(tiles)]
            rows.append(jnp.zeros((C - 8 * tiles, C), jnp.float32))
            fold_ref[h, pl.ds(8, C), :] = jnp.transpose(jnp.concatenate(rows, axis=0))
            offset = 8 if h else 8 + w - PAD
            moved = [
                pltpu.roll(fold_ref[h, pl.ds(offset + p * w, PAD), :], 8 * p, axis=1)
                for p in range(planes)
            ]
            for t in range(tiles):
                block = moved[0]
                for p in range(1, planes):
                    block = jnp.where(group == (t + p) % (C // 8), moved[p], block)
                target[t, pl.ds((PAD + C) * h, PAD), :] = pltpu.roll(block, (C - 8 * t) % C, axis=1)

    def arrive(whole, make, landed):
        for i, (dz, dm) in enumerate(DIRS):
            if dz == 0:
                when(-dm, lambda i=i: make(i).wait_recv())
        turn(whole, turned_in)
        for i, (dz, dm) in enumerate(DIRS):
            if dz != 0:
                when(-dm, lambda i=i: make(i).wait_recv())
        unfold(landed, turned_in)

    land_all(DIRS, bottom_copy)
    land_all(SIDES, state_copy)
    for k, dm, row in ((0, -1, 7), (1, 1, 8 + R)):
        def edge_in(k=k, row=row):
            for q in range(fields * half):
                state[q, pl.ds(row, 1), :] = state_rows_in[k, pl.ds(q, 1), :]
        def edge_none(row=row):
            for q in range(fields * half):
                state[q, pl.ds(row, 1), :] = jnp.zeros((1, C), jnp.float32)
        pl.when(has[dm])(edge_in)
        pl.when(jnp.logical_not(has[dm]))(edge_none)

    def neighbours(tile, before, after):
        east = jnp.where(lane_r == C - 1, after, pltpu.roll(tile, C - 1, axis=1))
        west = jnp.where(lane_r == 0, before, pltpu.roll(tile, 1, axis=1))
        return east, west

    deep = bottom[pl.ds(PAD, R), :]
    east_bottom, west_bottom = neighbours(
        deep,
        pltpu.roll(bottom_side[0, pl.ds(PAD, R), :], 1, axis=1),
        pltpu.roll(bottom_side[1, pl.ds(PAD, R), :], C - 1, axis=1),
    )

    def step_level(j, carry):
        level = g * half + j
        wet_c = (deep > level).astype(jnp.float32)
        wet_e = (east_bottom > level).astype(jnp.float32)
        wet_w = (west_bottom > level).astype(jnp.float32)
        wet_n = (bottom[pl.ds(PAD + 1, R), :] > level).astype(jnp.float32)
        wet_s = (bottom[pl.ds(PAD - 1, R), :] > level).astype(jnp.float32)
        vel_x = state[2 * half + j, pl.ds(8, R), :]
        vel_y = state[3 * half + j, pl.ds(8, R), :]
        for f in range(fields):
            q = f * half + j
            centre = state[q, pl.ds(8, R), :]
            east, west = neighbours(
                centre,
                pltpu.roll(state_cols_in[0], lax.rem(C - q, C), axis=1),
                pltpu.roll(state_cols_in[1], C - 1 - q, axis=1),
            )
            north = state[q, pl.ds(9, R), :]
            south = state[q, pl.ds(7, R), :]
            grad_x = 0.5 * (wet_e * east - wet_w * west)
            grad_y = 0.5 * (wet_n * north - wet_s * south)
            flux = wet_c * (
                wet_e * (east - centre) + wet_w * (west - centre)
                + wet_n * (north - centre) + wet_s * (south - centre)
            )
            back[q] = wet_c * (
                centre - ADVECTION * (vel_x * grad_x + vel_y * grad_y) + MIXING * flux
            )
        return carry

    lax.fori_loop(0, half, step_level, 0)
    share = pair * half
    give = pltpu.make_async_remote_copy(
        src_ref=back.at[pl.ds((1 - g) * share, share)], dst_ref=back_in,
        send_sem=bg_send, recv_sem=bg_recv, device_id=(1 - g, z, m), device_id_type=MESH)
    give.start()

    def stencil(source, emit):
        def column(k):
            return [source[t, k] for t in range(tiles)]

        first = column(0)
        before = [pltpu.roll(v, 1, axis=0) for v in column(columns - 1)]
        here = first
        for k in range(columns):
            if k < columns - 1:
                after = column(k + 1)
            else:
                after = [pltpu.roll(v, 7, axis=0) for v in first]
            south = pltpu.roll(here[tiles - 1], 1, axis=1)
            north = pltpu.roll(here[0], C - 1, axis=1)
            for t in range(tiles):
                below = here[t - 1] if t else south
                above = here[t + 1] if t < tiles - 1 else north
                emit(t, k, here[t], (before[t] + after[t]) + (below + above))
            before, here = here, after

    def depth_of(parts):
        stacked = jnp.concatenate(
            parts + [jnp.zeros((C - 8 * tiles, C), jnp.float32)], axis=0)
        return jnp.transpose(stacked).astype(jnp.bfloat16)

    depth_main = depth_of([bottom[strided(t), :].astype(jnp.float32) for t in range(tiles)])
    depth_side = depth_of([
        jnp.where(lane < C // 2, bottom_side[1, strided(t), :], bottom_side[0, strided(t), :])
        .astype(jnp.float32) for t in range(tiles)])
    row_c = lax.broadcasted_iota(jnp.int32, (C, C), 0)
    chunk = jnp.bitwise_and(lax.broadcasted_iota(jnp.int32, (C, C), 1), 7)
    for t in range(tiles):
        copy_of = jnp.where(row_c == chunk + 8 * t, 1.0, 0.0).astype(jnp.bfloat16)
        main = jnp.dot(depth_main, copy_of, preferred_element_type=jnp.float32)
        beyond = jnp.dot(depth_side, copy_of, preferred_element_type=jnp.float32)
        depth_ref[t, pl.ds(PAD, C), :] = main
        depth_ref[t, pl.ds(0, PAD), :] = beyond[C - PAD:]
        depth_ref[t, pl.ds(PAD + C, PAD), :] = beyond[:PAD]
    lane_level = lax.rem(lax.shift_right_logical(lane, jnp.full_like(lane, 3)), jnp.full_like(lane, levels))
    lane_level = lane_level.astype(jnp.float32)
    for t in range(tiles):
        for k in range(columns):
            ping[t, k] = jnp.where(depth_ref[t, strided_column(k), :] > lane_level, 1.0, 0.0)

    def coefficients(t, k, wet, near):
        gain = SMOOTHING * wet
        gain_ref[t, k] = gain
        keep_ref[t, k] = wet - gain * near

    stencil(ping, coefficients)

    def smooth(source):
        for t in range(tiles):
            for k in range(columns):
                ping[t, k] = jnp.where(gain_ref[t, k] > 0.0, source[t, strided_column(k), :], 0.0)

        def into(target):
            def emit(t, k, v, near):
                target[t, k] = keep_ref[t, k] * v + gain_ref[t, k] * near
            return emit

        def twice(i, carry):
            stencil(ping, into(pong))
            stencil(pong, into(ping))
            return carry

        lax.fori_loop(0, SWEEPS // 2, twice, 0)
        for t in range(tiles):
            for k in range(columns):
                turned_out[t, strided_column(k), :] = ping[t, k]
        turn_back(smooth_ref)

    arrive(field, one_copy, strips)
    smooth(turned_in)
    load_std.wait()
    give.wait_recv()

    def collect(j, carry):
        for f in range(pair):
            for other in range(2):
                if other:
                    p = f * levels + (1 - g) * half + j
                    prior = back_in[f * half + j]
                else:
                    p = f * levels + g * half + j
                    prior = back[(g * pair + f) * half + j]
                x_ref[pl.ds(pl.multiple_of(p * R, R), R), :] = (
                    std[p] * smooth_ref[p, pl.ds(PAD, R), :] + prior)
        return carry

    lax.fori_loop(0, half, collect, 0)
    total = planes * R
    x_ref[pl.ds(total, 8), :] = jnp.zeros((8, C), jnp.float32)
    both = jnp.concatenate([x_ref[pl.ds(0, total), :], x_ref[pl.ds(1, total), :]], axis=1)
    hot = rows_hot[...]
    picked = sum(jnp.dot(hot, part, preferred_element_type=jnp.float32) for part in pieces(both))
    corner_w = corner_hot[...]
    observed = jnp.sum(picked * corner_w, axis=1, keepdims=True)
    misfit = scale * (observed - seen)
    spread = pieces(corner_w * misfit)
    hot_t = rows_hot_t[...]
    scattered = sum(jnp.dot(hot_t, part, preferred_element_type=jnp.float32) for part in spread)
    x_ref[pl.ds(0, total), :] = scattered[:, :C] + pltpu.roll(scattered[:, C:], 1, axis=0)

    def weigh(p, carry):
        wet = deep > lax.rem(p, levels)
        adjoint = x_ref[pl.ds(pl.multiple_of(p * R, R), R), :]
        field_two[p, pl.ds(PAD, R), :] = jnp.where(wet, std[p] * adjoint, 0.0)
        return carry

    lax.fori_loop(0, planes, weigh, 0)
    pack(field_two, strips_out_two)
    start_all(DIRS, two_copy)
    arrive(field_two, two_copy, strips_two)
    smooth(turned_in)

    def write(p, carry):
        out_ref[p] = smooth_ref[p, pl.ds(PAD, R), :]
        return carry

    lax.fori_loop(0, planes, write, 0)
    sent_all(DIRS, bottom_copy)
    sent_all(SIDES, state_copy)
    sent_all(DIRS, one_copy)
    sent_all(DIRS, two_copy)
    give.wait_send()


def body(
    model_state,
    control,
    error_std,
    bottom_level,
    obs_count,
    obs_corner,
    obs_weight,
    obs_value,
    obs_precision,
    *,
    n_zon,
    n_mer,
):
    fields, half, R, C = model_state.shape
    pair, levels = control.shape[:2]
    planes = pair * levels
    slots = obs_corner.shape[-1]
    tiles = (R + 2 * SWEEPS + 7) // 8
    ext = R + 2 * PAD
    state_planes = fields * half
    f32 = jnp.float32
    turned = pltpu.VMEM((tiles, C + 2 * PAD, C), f32)
    slabs = pltpu.VMEM((tiles, (C + 2 * SWEEPS + 7) // 8, 8, C), f32)
    vmem = pl.BlockSpec(memory_space=pltpu.VMEM)
    hbm = pl.BlockSpec(memory_space=pl.ANY)
    dma = pltpu.SemaphoreType.DMA
    sizes = (n_zon, n_mer, levels, half, pair, fields, R, C)
    row_slots = (state_planes + 7) // 8 * 8
    smoothed = pl.pallas_call(
        functools.partial(kernel, sizes),
        out_shape=pltpu.VMEM((planes, R, C), f32),
        in_specs=[hbm] * 9,
        out_specs=vmem,
        scratch_shapes=[
            pltpu.VMEM((R, C), jnp.int32),
            pltpu.VMEM((1, 1), jnp.int32),
            pltpu.VMEM((1, slots), jnp.int32),
            pltpu.VMEM((4, slots), f32),
            pltpu.VMEM((1, slots), f32),
            pltpu.VMEM((1, slots), f32),
            pltpu.VMEM((state_planes, R + 16, C), f32),
            pltpu.VMEM((2, row_slots, C), f32),
            pltpu.VMEM((2, row_slots, C), f32),
            pltpu.VMEM((2, R, C), f32),
            pltpu.VMEM((2, R, C), f32),
            pltpu.VMEM((state_planes, R, C), f32),
            pltpu.VMEM((pair * half, R, C), f32),
            pltpu.VMEM((planes, ext, C), f32),
            turned,
            pltpu.VMEM((2, R, C), f32),
            pltpu.VMEM((2, ext, C), f32),
            pltpu.VMEM((planes, ext, C), f32),
            pltpu.VMEM((2, R, C), f32),
            pltpu.VMEM((2, ext, C), f32),
            pltpu.VMEM((2, C + PAD, C), f32),
            turned,
            turned,
            slabs,
            slabs,
            pltpu.VMEM((ext, C), jnp.int32),
            pltpu.VMEM((2, ext, C), jnp.int32),
            slabs,
            slabs,
            pltpu.VMEM((planes, R, C), f32),
            pltpu.VMEM((planes, ext, C), f32),
            pltpu.VMEM((planes * R + 8, C), f32),
            pltpu.VMEM((slots, planes * R), jnp.bfloat16),
            pltpu.VMEM((planes * R, slots), jnp.bfloat16),
            pltpu.VMEM((128, slots), f32),
            pltpu.VMEM((slots, 2 * C), f32),
            dma((9,)),
            dma((8,)), dma((8,)),
            dma((4,)), dma((4,)),
            dma((8,)), dma((8,)),
            dma((8,)), dma((8,)),
            dma, dma,
        ],
        compiler_params=pltpu.CompilerParams(collective_id=0, has_side_effects=True),
    )(
        model_state.reshape(state_planes, R, C),
        control.reshape(planes, R, C),
        error_std.reshape(planes, R, C),
        bottom_level,
        obs_count.reshape(1, 1),
        obs_corner.reshape(1, slots),
        obs_weight.reshape(4, slots),
        obs_value.reshape(1, slots),
        obs_precision.reshape(1, slots),
    )
    return control + smoothed.reshape(control.shape)


def solution(mesh):
    return jax.shard_map(
        functools.partial(body, n_zon=mesh.shape["zon"], n_mer=mesh.shape["mer"]),
        mesh=mesh,
        in_specs=(
            P(None, "grp", "mer", "zon"),
            P("grp", None, "mer", "zon"),
            P("grp", None, "mer", "zon"),
            P("mer", "zon"),
            P("grp", "mer", "zon"),
            P("grp", "mer", "zon", None),
            P("grp", "mer", "zon", None, None),
            P("grp", "mer", "zon", None),
            P("grp", "mer", "zon", None),
        ),
        out_specs=P("grp", None, "mer", "zon"),
        check_vma=False,
    )
```

profile of v0, /device:TPU:0, one launch (start us, length us, event | category | flops | bytes accessed | tf_op | source)
XLA Modules:
  0.0 29.0 jit_solution(6009968929732992702)
XLA Ops:
  0.7 0.0 copy-start
  0.7 27.5 %shard_map.91 = f32[12,64,128]{2,1,0:T(8,128)S(1)} custom-call(f32[12,64,128]{2,1,0:T(8,128)} %bitcast.12, f32[12,64,128]{2,1,0:T(8,128)} %bitcast.11, f32[12,64,128]{2,1,0:T(8,128)} %bitcast.13, s32[64,128]{1,0:T(8,128)} %bottom_hbm.1, s32[1,1]{1,0:T(1,128)} %bitcast.9.count_hbm, s32[1,256]{1,0:T(1,128)} %bitcast.15, f32[4,256]{1,0:T(4,128)} %bitcast.14, ...), custom_call_target="tpu_custom_call" | custom-call | tf_op jit(solution)/shard_map/pallas_call | solution.py:545
  28.2 0.0 copy-done
  28.2 0.8 %add.3 = f32[2,6,64,128]{3,2,1,0:T(8,128)} add(f32[2,6,64,128]{3,2,1,0:T(8,128)S(1)} %copy-done, f32[2,6,64,128]{3,2,1,0:T(8,128)S(1)} %bitcast.10) | non-fusion elementwise | flops 98304 | bytes 1179648 | tf_op jit(solution)/shard_map/add | solution.py:606
Async XLA Ops:
  0.7 27.5 %copy-start = (f32[2,6,64,128]{3,2,1,0:T(8,128)S(1)}, f32[2,6,64,128]{3,2,1,0:T(8,128)}, u32[]{:S(2)}) copy-start(f32[2,6,64,128]{3,2,1,0:T(8,128)} %param.10) | copy-start | bytes 1179652
where the time goes:
time: 29.1 us; the launch traced here: 29 us
  Pallas kernels  27.5 us (95%)
  other arithmetic  0.79 us (3%)
  between operations  0.68 us (2%)
    pallas_call x1, Pallas kernels, body(): pl.pallas_call(functools.partial(kernel, sizes), out_shape=pltpu.VMEM((pl...  27.5 us
    add x1, other arithmetic, body(): return control + smoothed.reshape(control.shape)  0.79 us

commit v1 on v0

v1 whole, which is shorter than its diff:
```python
import functools

import jax
import jax.numpy as jnp
from jax import lax
from jax.experimental import pallas as pl
from jax.experimental.pallas import tpu as pltpu
from jax.sharding import PartitionSpec as P

SWEEPS = 10
SMOOTHING = 0.2
ADVECTION = 0.1
MIXING = 0.15

MESH = pl.DeviceIdType.MESH
PAD = 16
ZONAL = [(1, 0), (-1, 0)]
MERIDIONAL = [(0, 1), (0, -1)]
SIDES = ZONAL + MERIDIONAL
DIRS = [(1, 1), (1, -1), (-1, 1), (-1, -1)] + ZONAL + MERIDIONAL


def pieces(value):
    parts = []
    for _ in range(2):
        part = value.astype(jnp.bfloat16)
        parts.append(part)
        value = value - part.astype(jnp.float32)
    return parts


def plane_groups(planes, ext, C):
    groups, first, tile = [], 0, 0
    while first < planes:
        count = 1 << ((planes - first).bit_length() - 1)
        chunks = C // count
        groups.append((first, count, tile, chunks, ext // chunks))
        first, tile = first + count, tile + ext // chunks
    return groups


def kernel(
    sizes,
    state_hbm,
    control_hbm,
    std_hbm,
    bottom_hbm,
    count_hbm,
    corner_hbm,
    weight_hbm,
    value_hbm,
    precision_hbm,
    out_ref,
    bottom_ref,
    count_ref,
    corner_ref,
    weight_ref,
    value_ref,
    precision_ref,
    state,
    state_rows,
    state_rows_in,
    state_cols,
    state_cols_in,
    back,
    back_in,
    field,
    strips_out,
    strips,
    field_two,
    strips_out_two,
    strips_two,
    turned_in,
    turned_out,
    depth_ref,
    fold_ref,
    ping,
    pong,
    keep_ref,
    gain_ref,
    bottom,
    bottom_side,
    std,
    smooth_ref,
    x_ref,
    parts_ref,
    rows_hot,
    rows_hot_t,
    obs_stack,
    corner_hot,
    local_sem,
    bot_send,
    bot_recv,
    st_send,
    st_recv,
    one_send,
    one_recv,
    two_send,
    two_recv,
    bg_send,
    bg_recv,
):
    n_zon, n_mer, levels, half, pair, fields, R, C = sizes
    w = SWEEPS
    planes = pair * levels
    ext = R + 2 * PAD
    groups = plane_groups(planes, ext, C)
    total_tiles = sum(tiles for *_, tiles in groups)
    columns = (C + 2 * w + 7) // 8
    column_base = PAD - (8 * columns - C) // 2
    g = lax.axis_index("grp")
    z = lax.axis_index("zon")
    m = lax.axis_index("mer")
    has = {-1: m > 0, 1: m < n_mer - 1}

    def device(dz, dm):
        return (g, lax.rem(z + dz + n_zon, n_zon), m + dm)

    def when(dm, action):
        if dm == 0:
            action()
        else:
            pl.when(has[dm])(action)

    barrier = pltpu.get_barrier_semaphore()
    pl.semaphore_signal(barrier, inc=1, device_id=(1 - g, z, m), device_id_type=MESH)
    for dz, dm in DIRS:
        def greet(dz=dz, dm=dm):
            pl.semaphore_signal(barrier, inc=1, device_id=device(dz, dm), device_id_type=MESH)
        when(dm, greet)

    load_control = pltpu.make_async_copy(control_hbm, smooth_ref.at[:, pl.ds(PAD, R)], local_sem.at[0])
    load_state = pltpu.make_async_copy(state_hbm, state.at[:, pl.ds(8, R)], local_sem.at[1])
    load_std = pltpu.make_async_copy(std_hbm, std, local_sem.at[2])
    load_bottom = pltpu.make_async_copy(bottom_hbm, bottom_ref, local_sem.at[3])
    tables = [
        pltpu.make_async_copy(source, target, local_sem.at[4 + i])
        for i, (source, target) in enumerate([
            (count_hbm, count_ref),
            (corner_hbm, corner_ref),
            (weight_hbm, weight_ref),
            (value_hbm, value_ref),
            (precision_hbm, precision_ref),
        ])
    ]
    load_bottom.start()
    load_state.start()
    load_control.start()
    load_std.start()
    for table in tables:
        table.start()

    lane_r = lax.broadcasted_iota(jnp.int32, (R, C), 1)
    lane = lax.broadcasted_iota(jnp.int32, (8, C), 1)

    def pack(source, target):
        for r in range(R // 8):
            first = jnp.zeros((8, C), jnp.float32)
            last = jnp.zeros((8, C), jnp.float32)
            for p in range(planes):
                at = p * w
                here = (lane >= at) & (lane < at + w)
                u = source[p, pl.ds(PAD + 8 * r, 8), :]
                last = jnp.where(here, pltpu.roll(u, (at + w) % C, axis=1), last)
                first = jnp.where(here, pltpu.roll(u, at, axis=1), first)
            target[0, pl.ds(8 * r, 8), :] = last
            target[1, pl.ds(8 * r, 8), :] = first

    def span(dm):
        if dm == 0:
            return pl.ds(0, R), pl.ds(PAD, R)
        if dm == 1:
            return pl.ds(R - PAD, PAD), pl.ds(0, PAD)
        return pl.ds(0, PAD), pl.ds(PAD + R, PAD)

    def side(dz):
        return 0 if dz == 1 else 1

    def bottom_copy(i):
        dz, dm = DIRS[i]
        src, dst = span(dm)
        target = bottom.at[dst] if dz == 0 else bottom_side.at[side(dz), dst]
        return pltpu.make_async_remote_copy(
            src_ref=bottom_ref.at[src], dst_ref=target,
            send_sem=bot_send.at[i], recv_sem=bot_recv.at[i],
            device_id=device(dz, dm), device_id_type=MESH)

    def halo_copy(i, whole, packed, landed, send, recv):
        dz, dm = DIRS[i]
        src, dst = span(dm)
        if dz == 0:
            inner = pl.ds(PAD + R - w, w) if dm == 1 else pl.ds(PAD, w)
            outer = pl.ds(PAD - w, w) if dm == 1 else pl.ds(PAD + R, w)
            source, target = whole.at[:, inner], whole.at[:, outer]
        else:
            source, target = packed.at[side(dz), src], landed.at[side(dz), dst]
        return pltpu.make_async_remote_copy(
            src_ref=source, dst_ref=target, send_sem=send.at[i], recv_sem=recv.at[i],
            device_id=device(dz, dm), device_id_type=MESH)

    def one_copy(i):
        return halo_copy(i, field, strips_out, strips, one_send, one_recv)

    def two_copy(i):
        return halo_copy(i, field_two, strips_out_two, strips_two, two_send, two_recv)

    def state_copy(i):
        dz, dm = SIDES[i]
        if dz == 0:
            k = 0 if dm == 1 else 1
            source, target = state_rows.at[k], state_rows_in.at[k]
        else:
            source, target = state_cols.at[side(dz)], state_cols_in.at[side(dz)]
        return pltpu.make_async_remote_copy(
            src_ref=source, dst_ref=target, send_sem=st_send.at[i], recv_sem=st_recv.at[i],
            device_id=device(dz, dm), device_id_type=MESH)

    def start_all(copies, make):
        for i, (dz, dm) in enumerate(copies):
            when(dm, lambda i=i: make(i).start())

    def land_all(copies, make):
        for i, (dz, dm) in enumerate(copies):
            when(-dm, lambda i=i: make(i).wait_recv())

    def sent_all(copies, make):
        for i, (dz, dm) in enumerate(copies):
            when(dm, lambda i=i: make(i).wait_send())

    load_bottom.wait()
    bottom[pl.ds(PAD, R)] = bottom_ref[...]
    for dm, rows in ((-1, pl.ds(0, PAD)), (1, pl.ds(PAD + R, PAD))):
        def dry(rows=rows):
            empty = jnp.zeros((PAD, C), jnp.int32)
            bottom[rows] = empty
            bottom_side[0, rows] = empty
            bottom_side[1, rows] = empty
            blank = jnp.zeros((PAD, C), jnp.float32)
            for landed in (strips, strips_two):
                landed[0, rows] = blank
                landed[1, rows] = blank

            def clear(p, carry):
                field[p, rows] = blank
                field_two[p, rows] = blank
                return carry

            lax.fori_loop(0, planes, clear, 0)
        pl.when(jnp.logical_not(has[dm]))(dry)

    load_state.wait()
    first = jnp.zeros((R, C), jnp.float32)
    last = jnp.zeros((R, C), jnp.float32)
    for q in range(fields * half):
        u = state[q, pl.ds(8, R), :]
        last = jnp.where(lane_r == q, pltpu.roll(u, (q + 1) % C, axis=1), last)
        first = jnp.where(lane_r == q, pltpu.roll(u, q, axis=1), first)
        state_rows[0, pl.ds(q, 1), :] = state[q, pl.ds(8 + R - 1, 1), :]
        state_rows[1, pl.ds(q, 1), :] = state[q, pl.ds(8, 1), :]
    state_cols[0] = last
    state_cols[1] = first

    edges = jnp.where(has[-1], 1, 0) + jnp.where(has[1], 1, 0)
    deep = bottom[pl.ds(PAD, R), :]
    load_control.wait()
    for p in range(planes):
        field[p, pl.ds(PAD, R), :] = jnp.where(
            deep > p % levels, smooth_ref[p, pl.ds(PAD, R), :], 0.0)
    pack(field, strips_out)
    pl.semaphore_wait(barrier, 3 + 3 * edges)
    start_all(DIRS, bottom_copy)
    start_all(SIDES, state_copy)
    start_all(DIRS, one_copy)

    for table in tables:
        table.wait()
    shift = C.bit_length() - 1
    slots = corner_ref.shape[1]
    corner = corner_ref[...]
    flat_row = lax.shift_right_logical(corner, jnp.full_like(corner, shift))
    column = corner - flat_row * C
    live = (lax.broadcasted_iota(jnp.int32, (1, slots), 1) < count_ref[...]).astype(jnp.float32)
    obs_stack[...] = jnp.zeros_like(obs_stack)
    obs_stack[pl.ds(0, 1), :] = column.astype(jnp.float32)
    obs_stack[pl.ds(1, 1), :] = flat_row.astype(jnp.float32)
    obs_stack[pl.ds(2, 4), :] = weight_ref[...]
    obs_stack[pl.ds(6, 1), :] = live * precision_ref[...]
    obs_stack[pl.ds(7, 1), :] = value_ref[...]
    turned = jnp.transpose(obs_stack[...])
    col_i = turned[:, 0:1].astype(jnp.int32)
    col_row = turned[:, 1:2].astype(jnp.int32)
    lane_s = lax.broadcasted_iota(jnp.int32, (slots, C), 1)
    here = lane_s == col_i
    beside = lane_s == col_i + 1
    for k in range(2):
        corner_hot[k] = jnp.where(here, turned[:, 2 + 2 * k:3 + 2 * k], 0.0) + jnp.where(
            beside, turned[:, 3 + 2 * k:4 + 2 * k], 0.0)
    scale = turned[:, 6:7]
    seen = turned[:, 7:8]

    def one_hot(k, carry):
        start = pl.multiple_of(k * C, C)
        ids = lax.broadcasted_iota(jnp.int32, (slots, C), 1) + k * C
        ids_t = lax.broadcasted_iota(jnp.int32, (C, slots), 0) + k * C
        for i in range(2):
            rows_hot[i * slots:(i + 1) * slots, pl.ds(start, C)] = jnp.where(
                ids == col_row + i, 1.0, 0.0).astype(jnp.bfloat16)
            rows_hot_t[pl.ds(start, C), i * slots:(i + 1) * slots] = jnp.where(
                ids_t == flat_row + i, 1.0, 0.0).astype(jnp.bfloat16)
        return carry

    lax.fori_loop(0, planes * R // C, one_hot, 0)

    def strided_column(k):
        return pl.ds(column_base + k, 8, columns)

    def turn(source):
        for first, count, tile, chunks, tiles in groups:
            for t in range(tiles):
                rows = [source[first + i, pl.ds(t, chunks, tiles), :] for i in range(count)]
                turned_in[tile + t, pl.ds(PAD, C), :] = jnp.transpose(
                    jnp.concatenate(rows, axis=0))

    def turn_back(target):
        for first, count, tile, chunks, tiles in groups:
            for t in range(tiles):
                rows = jnp.transpose(turned_out[tile + t, pl.ds(PAD, C), :])
                for i in range(count):
                    target[first + i, pl.ds(t, chunks, tiles), :] = rows[chunks * i:chunks * (i + 1)]

    lane_pad = lax.broadcasted_iota(jnp.int32, (PAD, C), 1)

    def unfold(landed):
        for h in range(2):
            for first, count, tile, chunks, tiles in groups:
                bits = chunks.bit_length() - 1
                group = lax.shift_right_logical(lane_pad, jnp.full_like(lane_pad, bits))
                rows = [landed[h, pl.ds(t, chunks, tiles), :] for t in range(tiles)]
                rows.append(jnp.zeros((C - chunks * tiles, C), jnp.float32))
                fold_ref[h, pl.ds(8, C), :] = jnp.transpose(jnp.concatenate(rows, axis=0))
                offset = 8 if h else 8 + w - PAD
                moved = [
                    pltpu.roll(fold_ref[h, pl.ds(offset + (first + i) * w, PAD), :], chunks * i, axis=1)
                    for i in range(count)
                ]
                for t in range(tiles):
                    block = moved[0]
                    for i in range(1, count):
                        block = jnp.where(group == (t + i) % count, moved[i], block)
                    turned_in[tile + t, pl.ds((PAD + C) * h, PAD), :] = pltpu.roll(
                        block, (C - chunks * t) % C, axis=1)

    def stencil(source, emit):
        for first, count, tile, chunks, tiles in groups:
            def column(k):
                return [source[tile + t, k] for t in range(tiles)]

            def lean(u, after):
                beyond = after[1:] + [pltpu.roll(after[0], C - 1, axis=1)]
                return [a + b for a, b in zip(u, beyond)]

            here = column(0)
            wrapped = [pltpu.roll(v, 7, axis=0) for v in here]
            slant_end = lean(column(columns - 1), wrapped)
            slant_before = [pltpu.roll(v, 1, axis=0) for v in slant_end]
            for k in range(columns):
                if k < columns - 1:
                    after = column(k + 1)
                    slant = lean(here, after)
                else:
                    slant = slant_end
                below = [pltpu.roll(slant[-1], 1, axis=1)] + slant[:-1]
                for t in range(tiles):
                    emit(tile + t, k, here[t], below[t] + slant_before[t])
                here, slant_before = after, slant

    def smooth():
        for t in range(total_tiles):
            for k in range(columns):
                ping[t, k] = turned_in[t, strided_column(k), :]

        def into(target):
            def emit(t, k, v, near):
                target[t, k] = keep_ref[t, k] * v + gain_ref[t, k] * near
            return emit

        def twice(i, carry):
            stencil(ping, into(pong))
            stencil(pong, into(ping))
            return carry

        lax.fori_loop(0, SWEEPS // 2, twice, 0)
        for t in range(total_tiles):
            for k in range(columns):
                turned_out[t, strided_column(k), :] = ping[t, k]
        turn_back(smooth_ref)

    def depth_of(rows_of):
        parts = []
        for first, count, tile, chunks, tiles in groups:
            rows = [rows_of(t, chunks, tiles).astype(jnp.float32) for t in range(tiles)]
            rows.append(jnp.zeros((C - chunks * tiles, C), jnp.float32))
            parts.append(jnp.transpose(jnp.concatenate(rows, axis=0)).astype(jnp.bfloat16))
        return parts

    row_c = lax.broadcasted_iota(jnp.int32, (C, C), 0)
    lane_c = lax.broadcasted_iota(jnp.int32, (C, C), 1)

    def spread_depth(parts, emit):
        for part, (first, count, tile, chunks, tiles) in zip(parts, groups):
            chunk = jnp.bitwise_and(lane_c, chunks - 1)
            for t in range(tiles):
                copy_of = jnp.where(row_c == chunk + chunks * t, 1.0, 0.0).astype(jnp.bfloat16)
                emit(tile + t, jnp.dot(part, copy_of, preferred_element_type=jnp.float32))

    lane_level = []
    for first, count, tile, chunks, tiles in groups:
        bits = chunks.bit_length() - 1
        plane = lax.shift_right_logical(lane, jnp.full_like(lane, bits)) + first
        level = jnp.where(plane >= levels, plane - levels, plane)
        lane_level += [level.astype(jnp.float32)] * tiles

    def coefficients():
        def main(t, value):
            depth_ref[t, pl.ds(PAD, C), :] = value

        def beside(t, n, step):
            east = bottom_side[1, pl.ds(t, n, step), :]
            west = bottom_side[0, pl.ds(t, n, step), :]
            at = lax.broadcasted_iota(jnp.int32, (n, C), 1)
            return jnp.where(at < C // 2, east, west)

        def sides(t, value):
            depth_ref[t, pl.ds(0, PAD), :] = value[C - PAD:]
            depth_ref[t, pl.ds(PAD + C, PAD), :] = value[:PAD]

        spread_depth(depth_of(lambda t, n, step: bottom[pl.ds(t, n, step), :]), main)
        spread_depth(depth_of(beside), sides)
        for t in range(total_tiles):
            for k in range(columns):
                pong[t, k] = jnp.where(
                    depth_ref[t, strided_column(k), :] > lane_level[t], 1.0, 0.0)

        def emit(t, k, wet, near):
            gain = SMOOTHING * wet
            gain_ref[t, k] = gain
            keep_ref[t, k] = wet - gain * near

        stencil(pong, emit)

    def meridional(copies, make, only):
        for i, (dz, dm) in enumerate(copies):
            if (dz == 0) == only:
                when(-dm, lambda i=i: make(i).wait_recv())

    share = pair * half
    give = pltpu.make_async_remote_copy(
        src_ref=back.at[pl.ds((1 - g) * share, share)], dst_ref=back_in,
        send_sem=bg_send, recv_sem=bg_recv, device_id=(1 - g, z, m), device_id_type=MESH)

    def model_step():
        land_all(SIDES, state_copy)
        for k, dm, row in ((0, -1, 7), (1, 1, 8 + R)):
            def edge_in(k=k, row=row):
                for q in range(fields * half):
                    state[q, pl.ds(row, 1), :] = state_rows_in[k, pl.ds(q, 1), :]
            def edge_none(row=row):
                for q in range(fields * half):
                    state[q, pl.ds(row, 1), :] = jnp.zeros((1, C), jnp.float32)
            pl.when(has[dm])(edge_in)
            pl.when(jnp.logical_not(has[dm]))(edge_none)

        def neighbours(tile, before, after):
            east = jnp.where(lane_r == C - 1, after, pltpu.roll(tile, C - 1, axis=1))
            west = jnp.where(lane_r == 0, before, pltpu.roll(tile, 1, axis=1))
            return east, west

        east_bottom, west_bottom = neighbours(
            deep,
            pltpu.roll(bottom_side[0, pl.ds(PAD, R), :], 1, axis=1),
            pltpu.roll(bottom_side[1, pl.ds(PAD, R), :], C - 1, axis=1),
        )

        def step_level(j, carry):
            level = g * half + j
            wet_c = (deep > level).astype(jnp.float32)
            wet_e = (east_bottom > level).astype(jnp.float32)
            wet_w = (west_bottom > level).astype(jnp.float32)
            wet_n = (bottom[pl.ds(PAD + 1, R), :] > level).astype(jnp.float32)
            wet_s = (bottom[pl.ds(PAD - 1, R), :] > level).astype(jnp.float32)
            vel_x = state[2 * half + j, pl.ds(8, R), :]
            vel_y = state[3 * half + j, pl.ds(8, R), :]
            for f in range(fields):
                q = f * half + j
                centre = state[q, pl.ds(8, R), :]
                east, west = neighbours(
                    centre,
                    pltpu.roll(state_cols_in[0], lax.rem(C - q, C), axis=1),
                    pltpu.roll(state_cols_in[1], C - 1 - q, axis=1),
                )
                north = state[q, pl.ds(9, R), :]
                south = state[q, pl.ds(7, R), :]
                grad_x = 0.5 * (wet_e * east - wet_w * west)
                grad_y = 0.5 * (wet_n * north - wet_s * south)
                flux = wet_c * (
                    wet_e * (east - centre) + wet_w * (west - centre)
                    + wet_n * (north - centre) + wet_s * (south - centre)
                )
                back[q] = wet_c * (
                    centre - ADVECTION * (vel_x * grad_x + vel_y * grad_y) + MIXING * flux
                )
            return carry

        lax.fori_loop(0, half, step_level, 0)
        give.start()

    meridional(DIRS, one_copy, True)
    turn(field)
    land_all(DIRS, bottom_copy)
    model_step()
    coefficients()
    meridional(DIRS, one_copy, False)
    unfold(strips)
    smooth()
    load_std.wait()
    give.wait_recv()

    def collect(j, carry):
        for f in range(pair):
            for other in range(2):
                if other:
                    p = f * levels + (1 - g) * half + j
                    prior = back_in[f * half + j]
                else:
                    p = f * levels + g * half + j
                    prior = back[(g * pair + f) * half + j]
                rows = pl.ds(pl.multiple_of(p * R, R), R)
                high, low = pieces(std[p] * smooth_ref[p, pl.ds(PAD, R), :] + prior)
                parts_ref[rows, :C] = high
                parts_ref[rows, C:] = low
        return carry

    lax.fori_loop(0, half, collect, 0)
    near_w = corner_hot[0]
    far_w = corner_hot[1]
    picked = jnp.dot(rows_hot[...], parts_ref[...], preferred_element_type=jnp.float32)
    picked = picked[:, :C] + picked[:, C:]
    observed = jnp.sum(picked[:slots] * near_w + picked[slots:] * far_w, axis=1, keepdims=True)
    misfit = scale * (observed - seen)
    spread = jnp.concatenate([near_w * misfit, far_w * misfit], axis=0)
    scattered = jnp.dot(
        rows_hot_t[...], jnp.concatenate(pieces(spread), axis=1), preferred_element_type=jnp.float32)
    x_ref[...] = scattered[:, :C] + scattered[:, C:]

    def weigh(p, carry):
        wet = deep > lax.rem(p, levels)
        adjoint = x_ref[pl.ds(pl.multiple_of(p * R, R), R), :]
        field_two[p, pl.ds(PAD, R), :] = jnp.where(wet, std[p] * adjoint, 0.0)
        return carry

    lax.fori_loop(0, planes, weigh, 0)
    pack(field_two, strips_out_two)
    start_all(DIRS, two_copy)
    meridional(DIRS, two_copy, True)
    turn(field_two)
    meridional(DIRS, two_copy, False)
    unfold(strips_two)
    smooth()

    def write(p, carry):
        out_ref[p] = smooth_ref[p, pl.ds(PAD, R), :]
        return carry

    lax.fori_loop(0, planes, write, 0)
    sent_all(DIRS, bottom_copy)
    sent_all(SIDES, state_copy)
    sent_all(DIRS, one_copy)
    sent_all(DIRS, two_copy)
    give.wait_send()


def body(
    model_state,
    control,
    error_std,
    bottom_level,
    obs_count,
    obs_corner,
    obs_weight,
    obs_value,
    obs_precision,
    *,
    n_zon,
    n_mer,
):
    fields, half, R, C = model_state.shape
    pair, levels = control.shape[:2]
    planes = pair * levels
    slots = obs_corner.shape[-1]
    ext = R + 2 * PAD
    state_planes = fields * half
    f32 = jnp.float32
    total_tiles = sum(tiles for *_, tiles in plane_groups(planes, ext, C))
    turned = pltpu.VMEM((total_tiles, C + 2 * PAD, C), f32)
    slabs = pltpu.VMEM((total_tiles, (C + 2 * SWEEPS + 7) // 8, 8, C), f32)
    vmem = pl.BlockSpec(memory_space=pltpu.VMEM)
    hbm = pl.BlockSpec(memory_space=pl.ANY)
    dma = pltpu.SemaphoreType.DMA
    sizes = (n_zon, n_mer, levels, half, pair, fields, R, C)
    row_slots = (state_planes + 7) // 8 * 8
    smoothed = pl.pallas_call(
        functools.partial(kernel, sizes),
        out_shape=pltpu.VMEM((planes, R, C), f32),
        in_specs=[hbm] * 9,
        out_specs=vmem,
        scratch_shapes=[
            pltpu.VMEM((R, C), jnp.int32),
            pltpu.VMEM((1, 1), jnp.int32),
            pltpu.VMEM((1, slots), jnp.int32),
            pltpu.VMEM((4, slots), f32),
            pltpu.VMEM((1, slots), f32),
            pltpu.VMEM((1, slots), f32),
            pltpu.VMEM((state_planes, R + 16, C), f32),
            pltpu.VMEM((2, row_slots, C), f32),
            pltpu.VMEM((2, row_slots, C), f32),
            pltpu.VMEM((2, R, C), f32),
            pltpu.VMEM((2, R, C), f32),
            pltpu.VMEM((state_planes, R, C), f32),
            pltpu.VMEM((pair * half, R, C), f32),
            pltpu.VMEM((planes, ext, C), f32),
            pltpu.VMEM((2, R, C), f32),
            pltpu.VMEM((2, ext, C), f32),
            pltpu.VMEM((planes, ext, C), f32),
            pltpu.VMEM((2, R, C), f32),
            pltpu.VMEM((2, ext, C), f32),
            turned,
            turned,
            turned,
            pltpu.VMEM((2, C + PAD, C), f32),
            slabs, slabs, slabs, slabs,
            pltpu.VMEM((ext, C), jnp.int32),
            pltpu.VMEM((2, ext, C), jnp.int32),
            pltpu.VMEM((planes, R, C), f32),
            pltpu.VMEM((planes, ext, C), f32),
            pltpu.VMEM((planes * R, C), f32),
            pltpu.VMEM((planes * R, 2 * C), jnp.bfloat16),
            pltpu.VMEM((2 * slots, planes * R), jnp.bfloat16),
            pltpu.VMEM((planes * R, 2 * slots), jnp.bfloat16),
            pltpu.VMEM((128, slots), f32),
            pltpu.VMEM((2, slots, C), f32),
            dma((9,)),
            dma((8,)), dma((8,)),
            dma((4,)), dma((4,)),
            dma((8,)), dma((8,)),
            dma((8,)), dma((8,)),
            dma, dma,
        ],
        compiler_params=pltpu.CompilerParams(collective_id=0, has_side_effects=True),
    )(
        model_state.reshape(state_planes, R, C),
        control.reshape(planes, R, C),
        error_std.reshape(planes, R, C),
        bottom_level,
        obs_count.reshape(1, 1),
        obs_corner.reshape(1, slots),
        obs_weight.reshape(4, slots),
        obs_value.reshape(1, slots),
        obs_precision.reshape(1, slots),
    )
    return control + smoothed.reshape(control.shape)


def solution(mesh):
    return jax.shard_map(
        functools.partial(body, n_zon=mesh.shape["zon"], n_mer=mesh.shape["mer"]),
        mesh=mesh,
        in_specs=(
            P(None, "grp", "mer", "zon"),
            P("grp", None, "mer", "zon"),
            P("grp", None, "mer", "zon"),
            P("mer", "zon"),
            P("grp", "mer", "zon"),
            P("grp", "mer", "zon", None),
            P("grp", "mer", "zon", None, None),
            P("grp", "mer", "zon", None),
            P("grp", "mer", "zon", None),
        ),
        out_specs=P("grp", None, "mer", "zon"),
        check_vma=False,
    )
```

time: 29.1 us -> 26.7 us (0.918)
  Pallas kernels: 27.5 us -> 25.1 us
    pallas_call x1, Pallas kernels: 27.5 us -> 25.1 us  [body(): pl.pallas_call(functools.partial(kernel, sizes), out_shape=pltpu.VMEM((pl...]
where the time goes in v1:
time: 26.7 us; the launch traced here: 26.6 us
  Pallas kernels  25.1 us (94%)
  other arithmetic  0.79 us (3%)
  between operations  0.68 us (3%)
    pallas_call x1, Pallas kernels, body(): pl.pallas_call(functools.partial(kernel, sizes), out_shape=pltpu.VMEM((pl...  25.1 us
    add x1, other arithmetic, body(): return control + smoothed.reshape(control.shape)  0.79 us

profile of v1, /device:TPU:0, one launch (start us, length us, event | category | flops | bytes accessed | tf_op | source)
XLA Modules:
  0.0 26.6 jit_solution(24960295031017949)
XLA Ops:
  0.7 0.0 copy-start
  0.7 25.1 %shard_map.91 = f32[12,64,128]{2,1,0:T(8,128)S(1)} custom-call(f32[12,64,128]{2,1,0:T(8,128)} %bitcast.12, f32[12,64,128]{2,1,0:T(8,128)} %bitcast.11, f32[12,64,128]{2,1,0:T(8,128)} %bitcast.13, s32[64,128]{1,0:T(8,128)} %bottom_hbm.1, s32[1,1]{1,0:T(1,128)} %bitcast.9.count_hbm, s32[1,256]{1,0:T(1,128)} %bitcast.15, f32[4,256]{1,0:T(4,128)} %bitcast.14, ...), custom_call_target="tpu_custom_call" | custom-call | tf_op jit(solution)/shard_map/pallas_call | solution.py:611
  25.8 0.0 copy-done
  25.8 0.8 %add.3 = f32[2,6,64,128]{3,2,1,0:T(8,128)} add(f32[2,6,64,128]{3,2,1,0:T(8,128)S(1)} %copy-done, f32[2,6,64,128]{3,2,1,0:T(8,128)S(1)} %bitcast.10) | non-fusion elementwise | flops 98304 | bytes 1179648 | tf_op jit(solution)/shard_map/add | solution.py:670
Async XLA Ops:
  0.7 25.1 %copy-start = (f32[2,6,64,128]{3,2,1,0:T(8,128)S(1)}, f32[2,6,64,128]{3,2,1,0:T(8,128)}, u32[]{:S(2)}) copy-start(f32[2,6,64,128]{3,2,1,0:T(8,128)} %param.10) | copy-start | bytes 1179652

commit v2 on v1

--- a/solution.py
+++ b/solution.py
@@ -16,7 +16,8 @@
 PAD = 16
 ZONAL = [(1, 0), (-1, 0)]
 MERIDIONAL = [(0, 1), (0, -1)]
-SIDES = ZONAL + MERIDIONAL
+LEDGE = 16
+GROUP = 32
 DIRS = [(1, 1), (1, -1), (-1, 1), (-1, -1)] + ZONAL + MERIDIONAL
 
 
@@ -60,8 +61,11 @@
     state,
     state_rows,
     state_rows_in,
-    state_cols,
-    state_cols_in,
+    edge_own,
+    edge_vel,
+    edge_in,
+    aux_out,
+    aux_in,
     back,
     back_in,
     field,
@@ -179,9 +183,12 @@
     def bottom_copy(i):
         dz, dm = DIRS[i]
         src, dst = span(dm)
-        target = bottom.at[dst] if dz == 0 else bottom_side.at[side(dz), dst]
+        if dz == 0:
+            source, target = bottom_ref.at[src], bottom.at[dst]
+        else:
+            source, target = aux_out.at[side(dz)], aux_in.at[3 * side(dz) + dm + 1]
         return pltpu.make_async_remote_copy(
-            src_ref=bottom_ref.at[src], dst_ref=target,
+            src_ref=source, dst_ref=target,
             send_sem=bot_send.at[i], recv_sem=bot_recv.at[i],
             device_id=device(dz, dm), device_id_type=MESH)
 
@@ -205,12 +212,9 @@
         return halo_copy(i, field_two, strips_out_two, strips_two, two_send, two_recv)
 
     def state_copy(i):
-        dz, dm = SIDES[i]
-        if dz == 0:
-            k = 0 if dm == 1 else 1
-            source, target = state_rows.at[k], state_rows_in.at[k]
-        else:
-            source, target = state_cols.at[side(dz)], state_cols_in.at[side(dz)]
+        dz, dm = MERIDIONAL[i]
+        k = 0 if dm == 1 else 1
+        source, target = state_rows.at[k], state_rows_in.at[k]
         return pltpu.make_async_remote_copy(
             src_ref=source, dst_ref=target, send_sem=st_send.at[i], recv_sem=st_recv.at[i],
             device_id=device(dz, dm), device_id_type=MESH)
@@ -257,8 +261,15 @@
         first = jnp.where(lane_r == q, pltpu.roll(u, q, axis=1), first)
         state_rows[0, pl.ds(q, 1), :] = state[q, pl.ds(8 + R - 1, 1), :]
         state_rows[1, pl.ds(q, 1), :] = state[q, pl.ds(8, 1), :]
-    state_cols[0] = last
-    state_cols[1] = first
+    fold = C // GROUP
+    depth_here = bottom_ref[...].astype(jnp.float32)
+    holds_depth = (lane_r >= LEDGE) & (lane_r < LEDGE + w)
+    edge_own[0] = jnp.where(holds_depth, pltpu.roll(depth_here, (LEDGE + w) % C, axis=1), last)
+    edge_own[1] = jnp.where(holds_depth, pltpu.roll(depth_here, LEDGE, axis=1), first)
+    for k in range(2):
+        aux_out[k] = sum(
+            pltpu.roll(edge_own[k, pl.ds(h * (R // fold), R // fold), :], GROUP * h, axis=1)
+            for h in range(fold))
 
     edges = jnp.where(has[-1], 1, 0) + jnp.where(has[1], 1, 0)
     deep = bottom[pl.ds(PAD, R), :]
@@ -269,7 +280,7 @@
     pack(field, strips_out)
     pl.semaphore_wait(barrier, 3 + 3 * edges)
     start_all(DIRS, bottom_copy)
-    start_all(SIDES, state_copy)
+    start_all(MERIDIONAL, state_copy)
     start_all(DIRS, one_copy)
 
     for table in tables:
@@ -420,10 +431,13 @@
         level = jnp.where(plane >= levels, plane - levels, plane)
         lane_level += [level.astype(jnp.float32)] * tiles
 
-    def coefficients():
+    def coefficients_main():
         def main(t, value):
             depth_ref[t, pl.ds(PAD, C), :] = value
 
+        spread_depth(depth_of(lambda t, n, step: bottom[pl.ds(t, n, step), :]), main)
+
+    def coefficients():
         def beside(t, n, step):
             east = bottom_side[1, pl.ds(t, n, step), :]
             west = bottom_side[0, pl.ds(t, n, step), :]
@@ -434,7 +448,6 @@
             depth_ref[t, pl.ds(0, PAD), :] = value[C - PAD:]
             depth_ref[t, pl.ds(PAD + C, PAD), :] = value[:PAD]
 
-        spread_depth(depth_of(lambda t, n, step: bottom[pl.ds(t, n, step), :]), main)
         spread_depth(depth_of(beside), sides)
         for t in range(total_tiles):
             for k in range(columns):
@@ -459,7 +472,7 @@
         send_sem=bg_send, recv_sem=bg_recv, device_id=(1 - g, z, m), device_id_type=MESH)
 
     def model_step():
-        land_all(SIDES, state_copy)
+        land_all(MERIDIONAL, state_copy)
         for k, dm, row in ((0, -1, 7), (1, 1, 8 + R)):
             def edge_in(k=k, row=row):
                 for q in range(fields * half):
@@ -470,16 +483,8 @@
             pl.when(has[dm])(edge_in)
             pl.when(jnp.logical_not(has[dm]))(edge_none)
 
-        def neighbours(tile, before, after):
-            east = jnp.where(lane_r == C - 1, after, pltpu.roll(tile, C - 1, axis=1))
-            west = jnp.where(lane_r == 0, before, pltpu.roll(tile, 1, axis=1))
-            return east, west
-
-        east_bottom, west_bottom = neighbours(
-            deep,
-            pltpu.roll(bottom_side[0, pl.ds(PAD, R), :], 1, axis=1),
-            pltpu.roll(bottom_side[1, pl.ds(PAD, R), :], C - 1, axis=1),
-        )
+        east_bottom = jnp.where(lane_r == C - 1, 0, pltpu.roll(deep, C - 1, axis=1))
+        west_bottom = jnp.where(lane_r == 0, 0, pltpu.roll(deep, 1, axis=1))
 
         def step_level(j, carry):
             level = g * half + j
@@ -493,11 +498,8 @@
             for f in range(fields):
                 q = f * half + j
                 centre = state[q, pl.ds(8, R), :]
-                east, west = neighbours(
-                    centre,
-                    pltpu.roll(state_cols_in[0], lax.rem(C - q, C), axis=1),
-                    pltpu.roll(state_cols_in[1], C - 1 - q, axis=1),
-                )
+                east = pltpu.roll(centre, C - 1, axis=1)
+                west = pltpu.roll(centre, 1, axis=1)
                 north = state[q, pl.ds(9, R), :]
                 south = state[q, pl.ds(7, R), :]
                 grad_x = 0.5 * (wet_e * east - wet_w * west)
@@ -512,12 +514,56 @@
             return carry
 
         lax.fori_loop(0, half, step_level, 0)
+        for k in range(2):
+            vel = edge_own[k]
+            speed = jnp.zeros((R, C), jnp.float32)
+            for f in range(fields):
+                speed = jnp.where(
+                    lane_r >= f * half, pltpu.roll(vel, (C + (f - 2) * half) % C, axis=1), speed)
+            edge_vel[k] = speed
+
+    def edge_step():
+        rows = R // fold
+        for k in range(2):
+            move = C - w - LEDGE if k == 0 else C - LEDGE
+            middle = aux_in[3 * k + 1]
+            for h in range(fold):
+                edge_in[k, pl.ds(h * rows, rows), :] = pltpu.roll(
+                    middle, (C - GROUP * h) % C, axis=1)
+                bottom_side[k, pl.ds(PAD + h * rows, rows), :] = pltpu.roll(
+                    middle, (C + move - GROUP * h) % C, axis=1).astype(jnp.int32)
+            for dm, h, start in ((1, fold - 1, 0), (-1, 0, PAD + R)):
+                def corner(dm=dm, h=h, start=start, k=k, move=move):
+                    bottom_side[k, pl.ds(start, rows), :] = pltpu.roll(
+                        aux_in[3 * k + dm + 1], (C + move - GROUP * h) % C, axis=1).astype(jnp.int32)
+                when(-dm, corner)
+        level_at = lane_r
+        for f in range(1, fields):
+            level_at = jnp.where(lane_r >= f * half, lane_r - f * half, level_at)
+        level_at = (level_at + g * half).astype(jnp.float32)
+        corrections = []
+        for k in range(2):
+            near_lane, own_lane = (LEDGE + w - 1, LEDGE) if k == 0 else (LEDGE, LEDGE + w - 1)
+            beyond = edge_in[k]
+            own = edge_own[1 - k]
+            both = (beyond[:, near_lane:near_lane + 1] > level_at) & (
+                own[:, own_lane:own_lane + 1] > level_at)
+            drift = (0.5 * ADVECTION if k == 0 else -0.5 * ADVECTION) * edge_vel[1 - k]
+            corrections.append(jnp.where(both, (MIXING + drift) * beyond - MIXING * own, 0.0))
+        for q in range(fields * half):
+            back[q] = back[q] + jnp.where(
+                lane_r == 0, pltpu.roll(corrections[0], (C - q) % C, axis=1),
+                jnp.where(
+                    lane_r == C - 1, pltpu.roll(corrections[1], C - 1 - q, axis=1), 0.0))
         give.start()
 
+    meridional(DIRS, bottom_copy, True)
+    model_step()
+    coefficients_main()
     meridional(DIRS, one_copy, True)
     turn(field)
-    land_all(DIRS, bottom_copy)
-    model_step()
+    meridional(DIRS, bottom_copy, False)
+    edge_step()
     coefficients()
     meridional(DIRS, one_copy, False)
     unfold(strips)
@@ -573,7 +619,7 @@
 
     lax.fori_loop(0, planes, write, 0)
     sent_all(DIRS, bottom_copy)
-    sent_all(SIDES, state_copy)
+    sent_all(MERIDIONAL, state_copy)
     sent_all(DIRS, one_copy)
     sent_all(DIRS, two_copy)
     give.wait_send()
@@ -625,6 +671,9 @@
             pltpu.VMEM((2, row_slots, C), f32),
             pltpu.VMEM((2, R, C), f32),
             pltpu.VMEM((2, R, C), f32),
+            pltpu.VMEM((2, R, C), f32),
+            pltpu.VMEM((2, R * GROUP // C, C), f32),
+            pltpu.VMEM((6, R * GROUP // C, C), f32),
             pltpu.VMEM((state_planes, R, C), f32),
             pltpu.VMEM((pair * half, R, C), f32),
             pltpu.VMEM((planes, ext, C), f32),
@@ -650,7 +699,7 @@
             pltpu.VMEM((2, slots, C), f32),
             dma((9,)),
             dma((8,)), dma((8,)),
-            dma((4,)), dma((4,)),
+            dma((2,)), dma((2,)),
             dma((8,)), dma((8,)),
             dma((8,)), dma((8,)),
             dma, dma,

time: 26.7 us -> 25.9 us (0.970)
  Pallas kernels: 25.1 us -> 24.3 us
    pallas_call x1, Pallas kernels: 25.1 us -> 24.3 us  [body(): pl.pallas_call(functools.partial(kernel, sizes), out_shape=pltpu.VMEM((pl...]
where the time goes in v2:
time: 25.9 us; the launch traced here: 25.8 us
  Pallas kernels  24.3 us (94%)
  other arithmetic  0.79 us (3%)
  between operations  0.68 us (3%)
    pallas_call x1, Pallas kernels, body(): pl.pallas_call(functools.partial(kernel, sizes), out_shape=pltpu.VMEM((pl...  24.3 us
    add x1, other arithmetic, body(): return control + smoothed.reshape(control.shape)  0.79 us

profile of v2, /device:TPU:0, one launch (start us, length us, event | category | flops | bytes accessed | tf_op | source)
XLA Modules:
  0.0 25.8 jit_solution(1525061023648754739)
XLA Ops:
  0.7 0.0 copy-start
  0.7 24.3 %shard_map.91 = f32[12,64,128]{2,1,0:T(8,128)S(1)} custom-call(f32[12,64,128]{2,1,0:T(8,128)} %bitcast.12, f32[12,64,128]{2,1,0:T(8,128)} %bitcast.11, f32[12,64,128]{2,1,0:T(8,128)} %bitcast.13, s32[64,128]{1,0:T(8,128)} %bottom_hbm.1, s32[1,1]{1,0:T(1,128)} %bitcast.9.count_hbm, s32[1,256]{1,0:T(1,128)} %bitcast.15, f32[4,256]{1,0:T(4,128)} %bitcast.14, ...), custom_call_target="tpu_custom_call" | custom-call | tf_op jit(solution)/shard_map/pallas_call | solution.py:657
  25.0 0.0 copy-done
  25.0 0.8 %add.3 = f32[2,6,64,128]{3,2,1,0:T(8,128)} add(f32[2,6,64,128]{3,2,1,0:T(8,128)S(1)} %copy-done, f32[2,6,64,128]{3,2,1,0:T(8,128)S(1)} %bitcast.10) | non-fusion elementwise | flops 98304 | bytes 1179648 | tf_op jit(solution)/shard_map/add | solution.py:719
Async XLA Ops:
  0.7 24.3 %copy-start = (f32[2,6,64,128]{3,2,1,0:T(8,128)S(1)}, f32[2,6,64,128]{3,2,1,0:T(8,128)}, u32[]{:S(2)}) copy-start(f32[2,6,64,128]{3,2,1,0:T(8,128)} %param.10) | copy-start | bytes 1179652

commit v3 on v2

--- a/solution.py
+++ b/solution.py
@@ -28,16 +28,6 @@
         parts.append(part)
         value = value - part.astype(jnp.float32)
     return parts
-
-
-def plane_groups(planes, ext, C):
-    groups, first, tile = [], 0, 0
-    while first < planes:
-        count = 1 << ((planes - first).bit_length() - 1)
-        chunks = C // count
-        groups.append((first, count, tile, chunks, ext // chunks))
-        first, tile = first + count, tile + ext // chunks
-    return groups
 
 
 def kernel(
@@ -74,10 +64,13 @@
     field_two,
     strips_out_two,
     strips_two,
+    mixed,
     turned_in,
     turned_out,
     depth_ref,
     fold_ref,
+    moved_ref,
+    owner_ref,
     ping,
     pong,
     keep_ref,
@@ -108,8 +101,9 @@
     w = SWEEPS
     planes = pair * levels
     ext = R + 2 * PAD
-    groups = plane_groups(planes, ext, C)
-    total_tiles = sum(tiles for *_, tiles in groups)
+    chunks = C // planes
+    tiles = (R + 2 * w + chunks - 1) // chunks
+    base = PAD - (chunks * tiles - R) // 2
     columns = (C + 2 * w + 7) // 8
     column_base = PAD - (8 * columns - C) // 2
     g = lax.axis_index("grp")
@@ -158,15 +152,15 @@
     lane = lax.broadcasted_iota(jnp.int32, (8, C), 1)
 
     def pack(source, target):
+        place = [(lane >= p * w) & (lane < p * w + w) for p in range(planes + 1)]
+        place[planes] = place[planes] | (lane < (planes + 1) * w - C)
         for r in range(R // 8):
             first = jnp.zeros((8, C), jnp.float32)
             last = jnp.zeros((8, C), jnp.float32)
             for p in range(planes):
-                at = p * w
-                here = (lane >= at) & (lane < at + w)
-                u = source[p, pl.ds(PAD + 8 * r, 8), :]
-                last = jnp.where(here, pltpu.roll(u, (at + w) % C, axis=1), last)
-                first = jnp.where(here, pltpu.roll(u, at, axis=1), first)
+                u = pltpu.roll(source[p, pl.ds(PAD + 8 * r, 8), :], (p * w + w) % C, axis=1)
+                last = jnp.where(place[p], u, last)
+                first = jnp.where(place[p + 1], u, first)
             target[0, pl.ds(8 * r, 8), :] = last
             target[1, pl.ds(8 * r, 8), :] = first
 
@@ -325,68 +319,77 @@
     def strided_column(k):
         return pl.ds(column_base + k, 8, columns)
 
+    def rows_at(t):
+        return pl.ds(base + t, chunks, tiles)
+
     def turn(source):
-        for first, count, tile, chunks, tiles in groups:
-            for t in range(tiles):
-                rows = [source[first + i, pl.ds(t, chunks, tiles), :] for i in range(count)]
-                turned_in[tile + t, pl.ds(PAD, C), :] = jnp.transpose(
-                    jnp.concatenate(rows, axis=0))
+        for t in range(tiles):
+            for p in range(planes):
+                mixed[t, pl.ds(chunks * p, chunks), :] = source[p, rows_at(t), :]
+            turned_in[t, pl.ds(PAD, C), :] = jnp.transpose(mixed[t])
 
     def turn_back(target):
-        for first, count, tile, chunks, tiles in groups:
-            for t in range(tiles):
-                rows = jnp.transpose(turned_out[tile + t, pl.ds(PAD, C), :])
-                for i in range(count):
-                    target[first + i, pl.ds(t, chunks, tiles), :] = rows[chunks * i:chunks * (i + 1)]
-
-    lane_pad = lax.broadcasted_iota(jnp.int32, (PAD, C), 1)
+        for t in range(tiles):
+            mixed[t] = jnp.transpose(turned_out[t, pl.ds(PAD, C), :])
+            for p in range(planes):
+                target[p, rows_at(t), :] = mixed[t, pl.ds(chunks * p, chunks), :]
+
+    def plane_of(at):
+        plane = jnp.zeros_like(at)
+        for p in range(1, planes):
+            plane = jnp.where(at >= chunks * p, p, plane)
+        return plane
+
+    for t in range(tiles):
+        owner_ref[t] = plane_of(jnp.bitwise_and(lane + (C - chunks * t), C - 1))
 
     def unfold(landed):
         for h in range(2):
-            for first, count, tile, chunks, tiles in groups:
-                bits = chunks.bit_length() - 1
-                group = lax.shift_right_logical(lane_pad, jnp.full_like(lane_pad, bits))
-                rows = [landed[h, pl.ds(t, chunks, tiles), :] for t in range(tiles)]
-                rows.append(jnp.zeros((C - chunks * tiles, C), jnp.float32))
-                fold_ref[h, pl.ds(8, C), :] = jnp.transpose(jnp.concatenate(rows, axis=0))
-                offset = 8 if h else 8 + w - PAD
-                moved = [
-                    pltpu.roll(fold_ref[h, pl.ds(offset + (first + i) * w, PAD), :], chunks * i, axis=1)
-                    for i in range(count)
-                ]
-                for t in range(tiles):
-                    block = moved[0]
-                    for i in range(1, count):
-                        block = jnp.where(group == (t + i) % count, moved[i], block)
-                    turned_in[tile + t, pl.ds((PAD + C) * h, PAD), :] = pltpu.roll(
+            for t in range(tiles):
+                mixed[h, pl.ds(chunks * t, chunks), :] = landed[h, rows_at(t), :]
+            folded = jnp.transpose(mixed[h])
+            fold_ref[h, pl.ds(8, C), :] = folded
+            fold_ref[h, pl.ds(8 + C, 8), :] = folded[:8]
+            offset = 8 + w if h else 8 + w - PAD
+            for p in range(planes):
+                moved_ref[h, p] = pltpu.roll(
+                    fold_ref[h, pl.ds(offset + p * w, PAD), :], chunks * p, axis=1)
+        for t in range(tiles):
+            owner = owner_ref[t]
+            mine = [owner == p for p in range(planes)]
+            for h in range(2):
+                for part in range(0, PAD, 8):
+                    block = moved_ref[h, 0, pl.ds(part, 8), :]
+                    for p in range(1, planes):
+                        block = jnp.where(mine[p], moved_ref[h, p, pl.ds(part, 8), :], block)
+                    turned_in[t, pl.ds((PAD + C) * h + part, 8), :] = pltpu.roll(
                         block, (C - chunks * t) % C, axis=1)
 
     def stencil(source, emit):
-        for first, count, tile, chunks, tiles in groups:
-            def column(k):
-                return [source[tile + t, k] for t in range(tiles)]
-
-            def lean(u, after):
-                beyond = after[1:] + [pltpu.roll(after[0], C - 1, axis=1)]
-                return [a + b for a, b in zip(u, beyond)]
-
-            here = column(0)
-            wrapped = [pltpu.roll(v, 7, axis=0) for v in here]
-            slant_end = lean(column(columns - 1), wrapped)
-            slant_before = [pltpu.roll(v, 1, axis=0) for v in slant_end]
-            for k in range(columns):
-                if k < columns - 1:
-                    after = column(k + 1)
-                    slant = lean(here, after)
-                else:
-                    slant = slant_end
-                below = [pltpu.roll(slant[-1], 1, axis=1)] + slant[:-1]
-                for t in range(tiles):
-                    emit(tile + t, k, here[t], below[t] + slant_before[t])
-                here, slant_before = after, slant
+        def column(k):
+            return [source[t, k] for t in range(tiles)]
+
+        def lean(u, after):
+            beyond = after[1:] + [pltpu.roll(after[0], C - 1, axis=1)]
+            return [a + b for a, b in zip(u, beyond)]
+
+        here = column(0)
+        wrapped = [pltpu.roll(v, 7, axis=0) for v in here]
+        slant_end = lean(column(columns - 1), wrapped)
+        slant_before = [pltpu.roll(v, 1, axis=0) for v in slant_end]
+        for k in range(columns):
+            if k < columns - 1:
+                after = column(k + 1)
+                slant = lean(here, after)
+            else:
+                slant = slant_end
+            below = [pltpu.roll(slant[-1], 1, axis=1)] + slant[:-1]
+            for t in range(tiles):
+                emit(t, k, here[t], below[t] + slant_before[t])
+            here, slant_before = after, slant
 
     def smooth():
-        for t in range(total_tiles):
+        for t in range(tiles):
             for k in range(columns):
                 ping[t, k] = turned_in[t, strided_column(k), :]
 
@@ -401,47 +404,41 @@
             return carry
 
         lax.fori_loop(0, SWEEPS // 2, twice, 0)
-        for t in range(total_tiles):
+        for t in range(tiles):
             for k in range(columns):
                 turned_out[t, strided_column(k), :] = ping[t, k]
         turn_back(smooth_ref)
 
     def depth_of(rows_of):
-        parts = []
-        for first, count, tile, chunks, tiles in groups:
-            rows = [rows_of(t, chunks, tiles).astype(jnp.float32) for t in range(tiles)]
-            rows.append(jnp.zeros((C - chunks * tiles, C), jnp.float32))
-            parts.append(jnp.transpose(jnp.concatenate(rows, axis=0)).astype(jnp.bfloat16))
-        return parts
+        for t in range(tiles):
+            mixed[0, pl.ds(chunks * t, chunks), :] = rows_of(rows_at(t)).astype(jnp.float32)
+        spare = C - chunks * tiles
+        mixed[0, pl.ds(chunks * tiles, spare), :] = jnp.zeros((spare, C), jnp.float32)
+        return jnp.transpose(mixed[0]).astype(jnp.bfloat16)
 
     row_c = lax.broadcasted_iota(jnp.int32, (C, C), 0)
     lane_c = lax.broadcasted_iota(jnp.int32, (C, C), 1)
-
-    def spread_depth(parts, emit):
-        for part, (first, count, tile, chunks, tiles) in zip(parts, groups):
-            chunk = jnp.bitwise_and(lane_c, chunks - 1)
-            for t in range(tiles):
-                copy_of = jnp.where(row_c == chunk + chunks * t, 1.0, 0.0).astype(jnp.bfloat16)
-                emit(tile + t, jnp.dot(part, copy_of, preferred_element_type=jnp.float32))
-
-    lane_level = []
-    for first, count, tile, chunks, tiles in groups:
-        bits = chunks.bit_length() - 1
-        plane = lax.shift_right_logical(lane, jnp.full_like(lane, bits)) + first
-        level = jnp.where(plane >= levels, plane - levels, plane)
-        lane_level += [level.astype(jnp.float32)] * tiles
+    chunk_c = lane_c - chunks * plane_of(lane_c)
+
+    def spread_depth(part, emit):
+        for t in range(tiles):
+            copy_of = jnp.where(row_c == chunk_c + chunks * t, 1.0, 0.0).astype(jnp.bfloat16)
+            emit(t, jnp.dot(part, copy_of, preferred_element_type=jnp.float32))
+
+    plane = plane_of(lane)
+    lane_level = jnp.where(plane >= levels, plane - levels, plane).astype(jnp.float32)
 
     def coefficients_main():
         def main(t, value):
             depth_ref[t, pl.ds(PAD, C), :] = value
 
-        spread_depth(depth_of(lambda t, n, step: bottom[pl.ds(t, n, step), :]), main)
+        spread_depth(depth_of(lambda rows: bottom[rows, :]), main)
 
     def coefficients():
-        def beside(t, n, step):
-            east = bottom_side[1, pl.ds(t, n, step), :]
-            west = bottom_side[0, pl.ds(t, n, step), :]
-            at = lax.broadcasted_iota(jnp.int32, (n, C), 1)
+        def beside(rows):
+            east = bottom_side[1, rows, :]
+            west = bottom_side[0, rows, :]
+            at = lax.broadcasted_iota(jnp.int32, (chunks, C), 1)
             return jnp.where(at < C // 2, east, west)
 
         def sides(t, value):
@@ -449,10 +446,10 @@
             depth_ref[t, pl.ds(PAD + C, PAD), :] = value[:PAD]
 
         spread_depth(depth_of(beside), sides)
-        for t in range(total_tiles):
+        for t in range(tiles):
             for k in range(columns):
                 pong[t, k] = jnp.where(
-                    depth_ref[t, strided_column(k), :] > lane_level[t], 1.0, 0.0)
+                    depth_ref[t, strided_column(k), :] > lane_level, 1.0, 0.0)
 
         def emit(t, k, wet, near):
             gain = SMOOTHING * wet
@@ -646,9 +643,10 @@
     ext = R + 2 * PAD
     state_planes = fields * half
     f32 = jnp.float32
-    total_tiles = sum(tiles for *_, tiles in plane_groups(planes, ext, C))
-    turned = pltpu.VMEM((total_tiles, C + 2 * PAD, C), f32)
-    slabs = pltpu.VMEM((total_tiles, (C + 2 * SWEEPS + 7) // 8, 8, C), f32)
+    chunks = C // planes
+    tiles = (R + 2 * SWEEPS + chunks - 1) // chunks
+    turned = pltpu.VMEM((tiles, C + 2 * PAD, C), f32)
+    slabs = pltpu.VMEM((tiles, (C + 2 * SWEEPS + 7) // 8, 8, C), f32)
     vmem = pl.BlockSpec(memory_space=pltpu.VMEM)
     hbm = pl.BlockSpec(memory_space=pl.ANY)
     dma = pltpu.SemaphoreType.DMA
@@ -682,10 +680,13 @@
             pltpu.VMEM((planes, ext, C), f32),
             pltpu.VMEM((2, R, C), f32),
             pltpu.VMEM((2, ext, C), f32),
+            pltpu.VMEM((tiles, C, C), f32),
             turned,
             turned,
             turned,
             pltpu.VMEM((2, C + PAD, C), f32),
+            pltpu.VMEM((2, planes, PAD, C), f32),
+            pltpu.VMEM((tiles, 8, C), jnp.int32),
             slabs, slabs, slabs, slabs,
             pltpu.VMEM((ext, C), jnp.int32),
             pltpu.VMEM((2, ext, C), jnp.int32),

time: 25.9 us -> 25.6 us (0.988)
  Pallas kernels: 24.3 us -> 24 us
    pallas_call x1, Pallas kernels: 24.3 us -> 24 us  [body(): pl.pallas_call(functools.partial(kernel, sizes), out_shape=pltpu.VMEM((pl...]
where the time goes in v3:
time: 25.6 us; the launch traced here: 25.4 us
  Pallas kernels  24 us (94%)
  other arithmetic  0.79 us (3%)
  between operations  0.68 us (3%)
    pallas_call x1, Pallas kernels, body(): pl.pallas_call(functools.partial(kernel, sizes), out_shape=pltpu.VMEM((pl...  24 us
    add x1, other arithmetic, body(): return control + smoothed.reshape(control.shape)  0.79 us

profile of v3, /device:TPU:0, one launch (start us, length us, event | category | flops | bytes accessed | tf_op | source)
XLA Modules:
  0.0 25.4 jit_solution(3878331006720993041)
XLA Ops:
  0.7 0.0 copy-start
  0.7 24.0 %shard_map.91 = f32[12,64,128]{2,1,0:T(8,128)S(1)} custom-call(f32[12,64,128]{2,1,0:T(8,128)} %bitcast.12, f32[12,64,128]{2,1,0:T(8,128)} %bitcast.11, f32[12,64,128]{2,1,0:T(8,128)} %bitcast.13, s32[64,128]{1,0:T(8,128)} %bottom_hbm.1, s32[1,1]{1,0:T(1,128)} %bitcast.9.count_hbm, s32[1,256]{1,0:T(1,128)} %bitcast.15, f32[4,256]{1,0:T(4,128)} %bitcast.14, ...), custom_call_target="tpu_custom_call" | custom-call | tf_op jit(solution)/shard_map/pallas_call | solution.py:655
  24.6 0.0 copy-done
  24.6 0.8 %add.3 = f32[2,6,64,128]{3,2,1,0:T(8,128)} add(f32[2,6,64,128]{3,2,1,0:T(8,128)S(1)} %copy-done, f32[2,6,64,128]{3,2,1,0:T(8,128)S(1)} %bitcast.10) | non-fusion elementwise | flops 98304 | bytes 1179648 | tf_op jit(solution)/shard_map/add | solution.py:720
Async XLA Ops:
  0.7 24.0 %copy-start = (f32[2,6,64,128]{3,2,1,0:T(8,128)S(1)}, f32[2,6,64,128]{3,2,1,0:T(8,128)}, u32[]{:S(2)}) copy-start(f32[2,6,64,128]{3,2,1,0:T(8,128)} %param.10) | copy-start | bytes 1179652

commit v4 on v3

--- a/solution.py
+++ b/solution.py
@@ -151,10 +151,10 @@
     lane_r = lax.broadcasted_iota(jnp.int32, (R, C), 1)
     lane = lax.broadcasted_iota(jnp.int32, (8, C), 1)
 
-    def pack(source, target):
+    def pack(source, target, blocks):
         place = [(lane >= p * w) & (lane < p * w + w) for p in range(planes + 1)]
         place[planes] = place[planes] | (lane < (planes + 1) * w - C)
-        for r in range(R // 8):
+        for r in blocks:
             first = jnp.zeros((8, C), jnp.float32)
             last = jnp.zeros((8, C), jnp.float32)
             for p in range(planes):
@@ -271,7 +271,7 @@
     for p in range(planes):
         field[p, pl.ds(PAD, R), :] = jnp.where(
             deep > p % levels, smooth_ref[p, pl.ds(PAD, R), :], 0.0)
-    pack(field, strips_out)
+    pack(field, strips_out, range(R // 8))
     pl.semaphore_wait(barrier, 3 + 3 * edges)
     start_all(DIRS, bottom_copy)
     start_all(MERIDIONAL, state_copy)
@@ -602,8 +602,16 @@
         return carry
 
     lax.fori_loop(0, planes, weigh, 0)
-    pack(field_two, strips_out_two)
-    start_all(DIRS, two_copy)
+    edge = PAD // 8
+    outer = [r for r in range(R // 8) if r < edge or r >= R // 8 - edge]
+    pack(field_two, strips_out_two, outer)
+    for i, (dz, dm) in enumerate(DIRS):
+        if dz != 0 and dm != 0:
+            when(dm, lambda i=i: two_copy(i).start())
+    pack(field_two, strips_out_two, [r for r in range(R // 8) if r not in outer])
+    for i, (dz, dm) in enumerate(DIRS):
+        if dz == 0 or dm == 0:
+            when(dm, lambda i=i: two_copy(i).start())
     meridional(DIRS, two_copy, True)
     turn(field_two)
     meridional(DIRS, two_copy, False)

time: 25.6 us -> 25.5 us (level)
  no operation moved by 1% of the time
where the time goes in v4:
time: 25.5 us; the launch traced here: 25.4 us
  Pallas kernels  23.9 us (94%)
  other arithmetic  0.79 us (3%)
  between operations  0.68 us (3%)
    pallas_call x1, Pallas kernels, body(): pl.pallas_call(functools.partial(kernel, sizes), out_shape=pltpu.VMEM((pl...  23.9 us
    add x1, other arithmetic, body(): return control + smoothed.reshape(control.shape)  0.79 us

profile of v4, /device:TPU:0, one launch (start us, length us, event | category | flops | bytes accessed | tf_op | source)
XLA Modules:
  0.0 25.4 jit_solution(512028991774892944)
XLA Ops:
  0.7 0.0 copy-start
  0.7 23.9 %shard_map.91 = f32[12,64,128]{2,1,0:T(8,128)S(1)} custom-call(f32[12,64,128]{2,1,0:T(8,128)} %bitcast.12, f32[12,64,128]{2,1,0:T(8,128)} %bitcast.11, f32[12,64,128]{2,1,0:T(8,128)} %bitcast.13, s32[64,128]{1,0:T(8,128)} %bottom_hbm.1, s32[1,1]{1,0:T(1,128)} %bitcast.9.count_hbm, s32[1,256]{1,0:T(1,128)} %bitcast.15, f32[4,256]{1,0:T(4,128)} %bitcast.14, ...), custom_call_target="tpu_custom_call" | custom-call | tf_op jit(solution)/shard_map/pallas_call | solution.py:663
  24.6 0.0 copy-done
  24.6 0.8 %add.3 = f32[2,6,64,128]{3,2,1,0:T(8,128)} add(f32[2,6,64,128]{3,2,1,0:T(8,128)S(1)} %copy-done, f32[2,6,64,128]{3,2,1,0:T(8,128)S(1)} %bitcast.10) | non-fusion elementwise | flops 98304 | bytes 1179648 | tf_op jit(solution)/shard_map/add | solution.py:728
Async XLA Ops:
  0.7 23.9 %copy-start = (f32[2,6,64,128]{3,2,1,0:T(8,128)S(1)}, f32[2,6,64,128]{3,2,1,0:T(8,128)}, u32[]{:S(2)}) copy-start(f32[2,6,64,128]{3,2,1,0:T(8,128)} %param.10) | copy-start | bytes 1179652
